TPU v7x, 512 devices: a whole 4x8x8 slice. The times are simulated.
512 devices in a mesh: wide: 64 (over y, z), narrow: 8 (over x, core).
Axes of the slice: x: 4, y: 8, z: 8, core: 2. Of those that a mesh axis runs over, the one named last changes fastest.
Arguments:
- hidden: bfloat16 [16384, 1536], P('wide', 'narrow'), may hold values from -6 to 6
- start_state: bfloat16 [1024, 24, 64, 128], P('wide', 'narrow'), may hold values from -0.59765625 to 0.59765625
- tail_inner: bfloat16 [1024, 3, 1536], P('wide', None, 'narrow'), may hold values from -6 to 6
- tail_shared: bfloat16 [1024, 3, 256], P('wide'), may hold values from -6 to 6
- input_gain: float32 [1536], replicated, may hold values from 0.5 to 1.5
- w_gate_inner: bfloat16 [1536, 3072], P(None, 'narrow'), may hold values from -0.15625 to 0.15625
- w_shared: bfloat16 [1536, 256], P(None, 'narrow'), may hold values from -0.15625 to 0.15625
- w_step: bfloat16 [1536, 24], P(None, 'narrow'), may hold values from -0.15625 to 0.15625
- step_bias: float32 [24], P('narrow'), may hold values from -4 to -1
- decay_log: float32 [24], P('narrow'), may hold values from 0 to 2.5
- conv_inner: bfloat16 [4, 1536], P(None, 'narrow'), may hold values from -3 to 3
- conv_inner_bias: float32 [1536], P('narrow'), may hold values from -1.5 to 1.5
- conv_shared: bfloat16 [4, 256], replicated, may hold values from -3 to 3
- conv_shared_bias: float32 [256], replicated, may hold values from -1.5 to 1.5
- skip_gain: float32 [24], P('narrow'), may hold values from 0.5 to 1.5
- gated_gain: float32 [1536], P('narrow'), may hold values from 0.5 to 1.5
- w_output: bfloat16 [1536, 1536], P('narrow'), may hold values from -0.15625 to 0.15625
- next_gain: float32 [1536], replicated, may hold values from 0.5 to 1.5
- w_next: bfloat16 [1536, 3224], P(None, 'narrow'), may hold values from -0.15625 to 0.15625
- dealing: int32 [1024], replicated, may hold values from 0 to 1023, as said below
- accepted: int32 [1024], replicated, may hold values from 0 to 16
- owners: int32 [1024], replicated, may hold values from 0 to 63, as said below
Outputs:
- new_hidden: bfloat16 [16384, 1536], P('wide', 'narrow')
- next_input: bfloat16 [16384, 3224], P('wide', 'narrow')
- kept_state: bfloat16 [1024, 24, 64, 128], P('wide', 'narrow')
- kept_tail_inner: bfloat16 [1024, 3, 1536], P('wide', None, 'narrow')
- kept_tail_shared: bfloat16 [1024, 3, 256], P('wide')
Inputs may be any that keep to these rules, and one draw needn't show every extreme that they name: `dealing`: a permutation of the 1024 requests; slot j lies on index j // 16 of wide. Each owner keeps exactly 16 requests, and the requests of the slots of one index of wide have different owners.
All inputs are finite; a program needn't handle non-finite values.
Results may differ from a plain program's by a relative error of at most 0.02.
Values may be sent and summed in bfloat16 or wider, within the bound.
A program may use at most 64 MiB of HBM per device.

v0:
```python
import jax
import jax.numpy as jnp
from jax import lax
from jax.sharding import PartitionSpec as P

EPSILON = 1e-05
HIGHEST = lax.Precision.HIGHEST


def root_norm(values, gain):
    values = values.astype(jnp.float32)
    factor = lax.rsqrt(jnp.mean(values * values, axis=-1, keepdims=True) + EPSILON)
    return (values * factor * gain).astype(jnp.bfloat16)


def causal_filter(tail, fresh, weight, offset):
    extended = jnp.concatenate([tail, fresh], axis=1)
    length = fresh.shape[1]
    summed = jnp.zeros(fresh.shape, jnp.float32) + offset
    for place in range(weight.shape[0]):
        summed = summed + extended[:, place : place + length].astype(jnp.float32) * weight[
            place
        ].astype(jnp.float32)
    return (jax.nn.silu(summed), extended)


def pick_rows(extended, accepted_now, count):
    length = extended.shape[1]
    wanted = accepted_now[:, None] + jnp.arange(count, dtype=jnp.int32)[None, :]
    onehot = (wanted[:, :, None] == jnp.arange(length, dtype=jnp.int32)[None, None, :]).astype(
        jnp.float32
    )
    return jnp.einsum(
        "rqe,rec->rqc", onehot, extended.astype(jnp.float32), precision=HIGHEST
    ).astype(jnp.bfloat16)


def state_block(
    inner, shared, step_raw, step_bias, decay_log, skip_gain, start_state, accepted_now
):
    states = shared.shape[-1] // 2
    b_part = shared[..., :states]
    c_part = shared[..., states:]
    length = inner.shape[1]
    steps_now = jax.nn.softplus(step_raw.astype(jnp.float32) + step_bias)
    log_decay = steps_now * -jnp.exp(decay_log)
    cumul = jnp.cumsum(log_decay, axis=1)
    prefix = jnp.concatenate([jnp.zeros_like(cumul[:, :1]), cumul], axis=1)
    places = jnp.arange(length, dtype=jnp.int32)
    lower = (places[:, None] >= places[None, :])[None, :, :, None]
    spread = cumul[:, :, None, :] - cumul[:, None, :, :]
    weights = (
        jnp.where(lower, jnp.exp(jnp.where(lower, spread, 0.0)), 0.0) * steps_now[:, None, :, :]
    )
    intersection = jnp.einsum("rtn,rsn->rts", c_part, b_part, precision=HIGHEST)
    mixing = weights * intersection[:, :, :, None]
    state_now = start_state.astype(jnp.float32)
    carried = (
        jnp.einsum("rtn,rhpn->rthp", c_part, state_now, precision=HIGHEST)
        * jnp.exp(cumul)[:, :, :, None]
    )
    direct = jnp.einsum("rtsh,rshp->rthp", mixing, inner, precision=HIGHEST)
    outputs = carried + direct + skip_gain[:, None] * inner
    chosen = (jnp.arange(length + 1, dtype=jnp.int32)[None, :] == accepted_now[:, None]).astype(
        jnp.float32
    )
    ending = jnp.einsum("rk,rkh->rh", chosen, prefix, precision=HIGHEST)
    before = (places[None, :] < accepted_now[:, None])[:, :, None]
    factor = (
        jnp.where(before, jnp.exp(jnp.where(before, ending[:, None, :] - cumul, 0.0)), 0.0)
        * steps_now
    )
    kept = jnp.exp(ending)[:, :, None, None] * state_now + jnp.einsum(
        "rsh,rshp,rsn->rhpn", factor, inner, b_part, precision=HIGHEST
    )
    return (outputs, kept.astype(jnp.bfloat16))


def local(
    hidden,
    start_state,
    tail_inner,
    tail_shared,
    input_gain,
    w_gate_inner,
    w_shared,
    w_step,
    step_bias,
    decay_log,
    conv_inner,
    conv_inner_bias,
    conv_shared,
    conv_shared_bias,
    skip_gain,
    gated_gain,
    w_output,
    next_gain,
    w_next,
    dealing,
    accepted,
    owners,
):
    wide_index = lax.axis_index("wide")
    wide_count = lax.axis_size("wide")
    narrow_count = lax.axis_size("narrow")
    full_rows = lax.all_gather(hidden, "narrow", axis=1, tiled=True)
    normed_in = root_norm(full_rows, input_gain)
    tokens = full_rows.shape[0]
    requests = start_state.shape[0]
    length = tokens // requests
    heads_here = w_step.shape[1]
    head_size = start_state.shape[2]
    block = w_output.shape[0]
    gate_inner = jnp.dot(normed_in, w_gate_inner, preferred_element_type=jnp.float32).astype(
        jnp.bfloat16
    )
    shared_piece = jnp.dot(normed_in, w_shared, preferred_element_type=jnp.float32).astype(
        jnp.bfloat16
    )
    step_raw = jnp.dot(normed_in, w_step, preferred_element_type=jnp.float32).astype(jnp.bfloat16)
    shared_in = lax.all_gather(shared_piece, "narrow", axis=1, tiled=True)
    gate_part = gate_inner[:, :block]
    inner_in = gate_inner[:, block:]
    inner_conv, inner_ext = causal_filter(
        tail_inner, inner_in.reshape(requests, length, block), conv_inner, conv_inner_bias
    )
    shared_conv, shared_ext = causal_filter(
        tail_shared, shared_in.reshape(requests, length, -1), conv_shared, conv_shared_bias
    )
    first_slot = wide_index * requests
    slot_requests = lax.dynamic_slice_in_dim(dealing, first_slot, requests)
    accepted_now = jnp.take(accepted, slot_requests)
    outputs, kept = state_block(
        inner_conv.reshape(requests, length, heads_here, head_size),
        shared_conv,
        step_raw.reshape(requests, length, heads_here),
        step_bias,
        decay_log,
        skip_gain,
        start_state,
        accepted_now,
    )
    gated = outputs.reshape(tokens, block) * jax.nn.silu(gate_part.astype(jnp.float32))
    squares = lax.psum(jnp.sum(gated * gated, axis=1, keepdims=True), "narrow")
    gated_norm = (
        gated * lax.rsqrt(squares / (block * narrow_count) + EPSILON) * gated_gain
    ).astype(jnp.bfloat16)
    partial_sum = jnp.dot(gated_norm, w_output, preferred_element_type=jnp.float32)
    whole_sum = lax.psum(partial_sum.astype(jnp.bfloat16), "narrow").astype(jnp.float32)
    new_full = (full_rows.astype(jnp.float32) + whole_sum).astype(jnp.bfloat16)
    new_part = lax.dynamic_slice_in_dim(
        new_full, lax.axis_index("narrow") * hidden.shape[1], hidden.shape[1], 1
    )
    normed_next = root_norm(new_full, next_gain)
    next_input = jnp.dot(normed_next, w_next, preferred_element_type=jnp.float32).astype(
        jnp.bfloat16
    )
    owner_table = (owners[:, None] == jnp.arange(wide_count, dtype=jnp.int32)[None, :]).astype(
        jnp.int32
    )
    ranking = jnp.sum((jnp.cumsum(owner_table, axis=0) - owner_table) * owner_table, axis=1)
    slot_owner = jnp.take(owners, dealing)
    slot_rank = jnp.take(ranking, dealing)
    local_owner = lax.dynamic_slice_in_dim(slot_owner, first_slot, requests)
    send_table = (jnp.arange(wide_count, dtype=jnp.int32)[:, None] == local_owner[None, :]).astype(
        jnp.bfloat16
    )
    state_bucket = (
        jnp.dot(send_table, kept.reshape(requests, -1), preferred_element_type=jnp.float32)
        .astype(jnp.bfloat16)
        .reshape((wide_count,) + kept.shape[1:])
    )
    inner_edge = pick_rows(inner_ext, accepted_now, tail_inner.shape[1])
    shared_edge = pick_rows(shared_ext, accepted_now, tail_shared.shape[1])
    inner_bucket = jnp.einsum(
        "or,rqc->oqc", send_table, inner_edge, preferred_element_type=jnp.float32
    ).astype(jnp.bfloat16)
    shared_bucket = jnp.einsum(
        "or,rqc->oqc", send_table, shared_edge, preferred_element_type=jnp.float32
    ).astype(jnp.bfloat16)
    state_recv, inner_recv, shared_recv = (
        lax.all_to_all(state_bucket, "wide", split_axis=0, concat_axis=0, tiled=True),
        lax.all_to_all(inner_bucket, "wide", split_axis=0, concat_axis=0, tiled=True),
        lax.all_to_all(shared_bucket, "wide", split_axis=0, concat_axis=0, tiled=True),
    )
    senders = jnp.arange(slot_owner.shape[0], dtype=jnp.int32) // requests
    mine = slot_owner == wide_index
    picking = (
        (slot_rank[:, None] == jnp.arange(requests, dtype=jnp.int32)[None, :]) & mine[:, None]
    ).astype(jnp.bfloat16)
    from_sender = (senders[:, None] == jnp.arange(wide_count, dtype=jnp.int32)[None, :]).astype(
        jnp.bfloat16
    )
    selector = jnp.einsum(
        "jk,jw->kw", picking, from_sender, preferred_element_type=jnp.float32
    ).astype(jnp.bfloat16)
    kept_state = (
        jnp.dot(selector, state_recv.reshape(wide_count, -1), preferred_element_type=jnp.float32)
        .astype(jnp.bfloat16)
        .reshape(start_state.shape)
    )
    kept_tail_inner = jnp.einsum(
        "kw,wqc->kqc", selector, inner_recv, preferred_element_type=jnp.float32
    ).astype(jnp.bfloat16)
    kept_tail_shared = jnp.einsum(
        "kw,wqc->kqc", selector, shared_recv, preferred_element_type=jnp.float32
    ).astype(jnp.bfloat16)
    return (new_part, next_input, kept_state, kept_tail_inner, kept_tail_shared)


def solution(mesh):
    placed = (
        P("wide", "narrow"),
        P("wide", "narrow", None, None),
        P("wide", None, "narrow"),
        P("wide", None, None),
        P(),
        P(None, "narrow"),
        P(None, "narrow"),
        P(None, "narrow"),
        P("narrow"),
        P("narrow"),
        P(None, "narrow"),
        P("narrow"),
        P(),
        P(),
        P("narrow"),
        P("narrow"),
        P("narrow", None),
        P(),
        P(None, "narrow"),
        P(),
        P(),
        P(),
    )
    return jax.shard_map(
        local,
        mesh=mesh,
        in_specs=placed,
        out_specs=(
            P("wide", "narrow"),
            P("wide", "narrow"),
            P("wide", "narrow", None, None),
            P("wide", None, "narrow"),
            P("wide", None, None),
        ),
        check_vma=False,
    )
```

profile of v0, /device:TPU:24, one launch (start us, length us, event | category | flops | bytes accessed | tf_op | source)
XLA Modules:
  0.0 219.7 jit_solution(16669502044702229559)
XLA Ops:
  7.2 0.8 fusion.81
  8.0 0.8 compare_select_fusion.2
  8.8 1.3 gather_fusion
  10.1 0.8 and_select_fusion
  10.9 4.5 %gather_fusion.2 = s32[1024]{0:T(1024)S(1)} fusion(s32[1024]{0:T(1024)S(1)} %copy-done.1, s32[1024]{0:T(1024)S(1)} %fusion.81), kind=kCustom, calls=%fused_computation.1.clone | custom fusion | bytes 12288 | tf_op jit(solution)/shard_map/jit(_take)/gather | solution.py:162
  15.4 0.6 broadcast_compare_fusion
  16.2 13.7 %all_gather.6 = bf16[256,1536]{0,1:T(8,128)(2,1)S(1)} all-gather(bf16[256,192]{0,1:T(8,128)(2,1)S(1)} %copy-done.7), channel_id=1, replica_groups=mesh['wide'=64,'narrow'=8] {'narrow'}, dimensions={1}, use_global_device_ids=true | all-gather | bytes 884736 | tf_op jit(solution)/shard_map/all_gather | solution.py:106
  29.9 0.3 copy.79
  30.2 0.2 fusion.6
  30.5 1.9 convolution_convert_fusion.4
  32.6 0.5 copy-done.6
  33.1 0.2 convolution_convert_fusion.8
  33.4 0.3 convolution_convert_fusion.6
  33.7 0.7 copy.98
  34.4 16.6 %all-to-all-start.1 = ((bf16[64,3,192]{2,1,0:T(4,128)(2,1)}), bf16[64,3,192]{2,1,0:T(4,128)(2,1)}, u32[]{:S(2)}, u32[]{:S(2)}) async-start(bf16[64,3,192]{2,1,0:T(4,128)(2,1)} %copy.98), calls=%async_computation.1 | async-start | bytes 262144 | tf_op jit(solution)/shard_map/all_to_all | solution.py:183
  51.2 0.6 slice_convert_fusion.7
  51.9 0.4 fusion.15
  52.3 0.4 convolution_convert_fusion.11
  52.8 0.1 broadcast_multiply_fusion.1
  52.9 0.2 copy.82
  53.1 0.7 fusion.90
  53.8 0.2 copy.94
  54.4 0.8 copy.95
  55.2 12.7 %all_gather.7 = bf16[256,256]{0,1:T(8,128)(2,1)S(1)} all-gather(bf16[256,32]{0,1:T(8,128)(2,1)S(1)} %convolution_convert_fusion.11), channel_id=1, replica_groups=mesh['wide'=64,'narrow'=8] {'narrow'}, dimensions={1}, use_global_device_ids=true | all-gather | bytes 147456 | tf_op jit(solution)/shard_map/all_gather | solution.py:121
  68.0 0.2 convolution_convert_fusion.7
  68.3 0.3 convolution_convert_fusion.5
  68.6 0.1 copy-done.5
  68.7 0.7 copy.101
  69.4 0.9 divide_multiply_fusion
  70.4 1.1 reshape.238
  71.5 2.2 %broadcast_multiply_fusion = f32[16,16,3,64]{3,2,1,0:T(4,128)} fusion(f32[16,16,3,64]{3,2,1,0:T(4,128)S(1)} %reshape.238, f32[16,16,3]{2,1,0:T(8,128)} %copy.95), kind=kLoop, calls=%fused_computation.72 | loop fusion | flops 49152 | bytes 396288 | tf_op jit(solution)/shard_map/rsh,rshp,rsn->rhpn/dot_general | solution.py:73
  73.7 1.5 divide_multiply_fusion.1
  75.2 12.7 %all-to-all-start.2 = ((bf16[64,3,256]{2,1,0:T(4,128)(2,1)}), bf16[64,3,256]{2,1,0:T(4,128)(2,1)S(1)}, u32[]{:S(2)}, u32[]{:S(2)}) async-start(bf16[64,3,256]{2,1,0:T(4,128)(2,1)} %copy.101), calls=%async_computation.2 | async-start | bytes 262144 | tf_op jit(solution)/shard_map/all_to_all | solution.py:184
  87.9 3.8 %add_convert_fusion = bf16[16,3,64,128]{3,2,1,0:T(8,128)(2,1)S(1)} fusion(bf16[16,3,64,128]{3,2,1,0:T(8,128)(2,1)S(1)} %copy-done.2, f32[16,3]{1,0:T(8,128)S(1)} %copy.93, f32[16,16,3,64]{3,2,1,0:T(4,128)} %broadcast_multiply_fusion, f32[16,16,256]{2,1,0:T(8,128)S(1)} %divide_multiply_fusion.1), kind=kOutput, calls=%fused_computation.21 | convolution fusion | flops 77070336 | bytes 1908736 | tf_op jit(solution)/shard_map/rsh,rshp,rsn->rhpn/dot_general | solution.py:73
  91.7 1.8 fusion.2
  93.5 2.5 %copy.114 = bf16[8,8,192,128]{3,2,1,0:T(8,128)(2,1)} copy(bf16[8,8,192,128]{3,1,2,0:T(8,128)(2,1)S(1)} %fusion.2) | data formatting | bytes 6291456
  96.0 2.8 %all-to-all-done.2 = bf16[64,3,256]{2,1,0:T(4,128)(2,1)S(1)} async-done(((bf16[64,3,256]{2,1,0:T(4,128)(2,1)}), bf16[64,3,256]{2,1,0:T(4,128)(2,1)S(1)}, u32[]{:S(2)}, u32[]{:S(2)}) %all-to-all-start.2) | async-done | bytes 98336 | tf_op jit(solution)/shard_map/all_to_all | solution.py:184
  98.8 10.3 %all-to-all-start = ((bf16[64,3,64,128]{3,2,1,0:T(8,128)(2,1)}), bf16[64,3,64,128]{3,2,1,0:T(8,128)(2,1)}, u32[]{:S(2)}, u32[]{:S(2)}) async-start(bf16[64,3,64,128]{3,2,1,0:T(8,128)(2,1)} %bitcast.87), calls=%async_computation | async-start | bytes 6291456 | tf_op jit(solution)/shard_map/all_to_all | solution.py:182
  109.1 0.6 copy.87
  109.7 0.8 copy.85
  110.5 0.2 copy.83
  110.8 0.3 fusion.59
  111.1 1.7 convolution_multiply_fusion
  112.9 0.6 fusion.14
  113.5 0.2 copy.90
  113.7 0.3 reshape.239
  114.0 1.1 multiply_reduce_fusion
  115.1 14.5 %psum.14 = f32[256,1]{0,1:T(1,128)S(1)} all-reduce(f32[256,1]{0,1:T(1,128)S(1)} %bitcast.96), channel_id=1, replica_groups=mesh['wide'=64,'narrow'=8] {'narrow'}, use_global_device_ids=true, to_apply=%region_3.4 | all-reduce | flops 256 | bytes 2048 | tf_op jit(solution)/shard_map/psum | solution.py:144
  129.7 2.4 %convolution_convert_fusion.2 = bf16[256,1536]{1,0:T(8,128)(2,1)} fusion(bf16[192,1536]{1,0:T(8,128)(2,1)} %param.40, f32[192]{0:T(256)S(1)} %copy-done.24, f32[256]{0:T(256)S(1)} %bitcast.105, f32[256,192]{1,0:T(8,128)S(1)} %reshape.239, bf16[256,384]{1,0:T(8,128)(2,1)} %copy-done.6), kind=kOutput, calls=%fused_computation.7 | convolution fusion | flops 151830528 | bytes 1705728 | tf_op jit(solution)/shard_map/dot_general | solution.py:148
  132.2 18.0 %reduce-window.6 = s32[64,8,128]{2,1,0:T(8,128)S(1)} reduce-window(s32[64,8,128]{2,1,0:T(8,128)S(1)} %fusion.41, s32[]{:T(128)} %constant.71.clone.1), window={size=1x1x128 pad=0_0x0_0x127_0}, to_apply=%region_6.7 | reduce-window | flops 8323072 | bytes 524292 | tf_op jit(solution)/shard_map/reduce-window
  150.2 0.1 slice.102
  150.3 0.1 copy.91
  150.6 0.1 broadcast_add_fusion
  150.8 4.5 %gather_fusion.1 = s32[1024]{0:T(1024)S(1)} fusion(s32[1024]{0:T(1024)S(1)} %fusion.37, s32[1024]{0:T(1024)S(1)} %fusion.81), kind=kCustom, calls=%fused_computation.clone | custom fusion | bytes 12288 | tf_op jit(solution)/shard_map/jit(_take)/gather | solution.py:163
  155.4 0.8 convolution_convert_fusion.12
  156.2 1.7 convolution_convert_fusion.10
  157.8 0.7 convolution_convert_fusion.9
  158.6 45.9 %all-reduce.3.cloned.1.call-done = bf16[256,1536]{1,0:T(8,128)(2,1)} async-done(((bf16[256,1536]{1,0:T(8,128)(2,1)}), bf16[256,1536]{1,0:T(8,128)(2,1)}) %all-reduce.3.cloned.1.call-update) | async-done | bytes 786448 | tf_op jit(solution)/shard_map/psum | solution.py:149
  204.5 1.5 fusion.3
  206.0 0.1 constant_dynamic-slice_fusion
  206.1 0.7 copy.103
  206.8 1.3 convolution_convert_fusion.3
  208.2 3.7 %fusion.10 = bf16[2,8,192,128]{3,1,2,0:T(8,128)(2,1)S(1)} fusion(bf16[16,64]{1,0:T(8,128)(2,1)S(1)} %convolution_convert_fusion.12, bf16[8,8,192,128]{3,2,1,0:T(8,128)(2,1)} %bitcast.34), kind=kOutput, calls=%fused_computation.22 | convolution fusion | flops 50724864 | bytes 3934208 | tf_op jit(solution)/shard_map/dot_general | solution.py:198
  211.8 1.0 copy.116
  (85 shorter events, 1.5 us)
Async XLA Ops:
  7.2 199.7 %copy-start = (bf16[1536,403]{0,1:T(8,128)(2,1)S(1)}, bf16[1536,403]{0,1:T(8,128)(2,1)}, u32[]{:S(2)}) copy-start(bf16[1536,403]{0,1:T(8,128)(2,1)} %param.42) | copy-start | bytes 3714052
  7.2 3.7 %copy-start.1 = (s32[1024]{0:T(1024)S(1)}, s32[1024]{0:T(1024)}, u32[]{:S(2)}) copy-start(s32[1024]{0:T(1024)} %param.45) | copy-start | bytes 12292
  10.9 4.6 %copy-start.12 = (s32[1024]{0:T(1024)S(1)}, s32[1024]{0:T(1024)}, u32[]{:S(2)}) copy-start(s32[1024]{0:T(1024)} %param.43) | copy-start | bytes 12292
  10.9 5.3 %copy-start.10 = (bf16[16,3,192]{2,0,1:T(8,128)(2,1)S(1)}, bf16[16,3,192]{2,0,1:T(8,128)(2,1)}, u32[]{:S(2)}) copy-start(bf16[16,3,192]{2,0,1:T(8,128)(2,1)} %param.26) | copy-start | bytes 55300
  10.9 5.3 %copy-start.7 = (bf16[256,192]{0,1:T(8,128)(2,1)S(1)}, bf16[256,192]{0,1:T(8,128)(2,1)}, u32[]{:S(2)}) copy-start(bf16[256,192]{0,1:T(8,128)(2,1)} %param.24) | copy-start | bytes 294916
  16.1 52.2 %copy-start.15 = (s32[16]{0:T(128)}, s32[16]{0:T(128)S(1)}, u32[]{:S(2)}) copy-start(s32[16]{0:T(128)S(1)} %dynamic_slice.10) | copy-start | bytes 196
  16.2 14.3 %copy-start.22 = (f32[1536]{0:T(1024)S(1)}, f32[1536]{0:T(1024)}, u32[]{:S(2)}) copy-start(f32[1536]{0:T(1024)} %param.28) | copy-start | bytes 18436
  30.5 20.7 %copy-start.25 = (f32[3]{0:T(128)S(1)}, f32[3]{0:T(128)}, u32[]{:S(2)}) copy-start(f32[3]{0:T(128)} %param.33) | copy-start | bytes 40
  30.5 20.7 %copy-start.13 = (bf16[4,192]{1,0:T(4,128)(2,1)S(1)}, bf16[4,192]{1,0:T(4,128)(2,1)}, u32[]{:S(2)}) copy-start(bf16[4,192]{1,0:T(4,128)(2,1)} %param.34) | copy-start | bytes 4612
  30.5 20.7 %copy-start.14 = (bf16[4,256]{1,0:T(4,128)(2,1)S(1)}, bf16[4,256]{1,0:T(4,128)(2,1)}, u32[]{:S(2)}) copy-start(bf16[4,256]{1,0:T(4,128)(2,1)} %param.36) | copy-start | bytes 6148
  30.5 21.4 %copy-start.11 = (bf16[16,3,256]{2,0,1:T(8,128)(2,1)S(1)}, bf16[16,3,256]{2,0,1:T(8,128)(2,1)}, u32[]{:S(2)}) copy-start(bf16[16,3,256]{2,0,1:T(8,128)(2,1)} %param.27) | copy-start | bytes 73732
  30.5 21.4 %copy-start.21 = (bf16[1536,3]{0,1:T(4,128)(2,1)S(1)}, bf16[1536,3]{0,1:T(4,128)(2,1)}, u32[]{:S(2)}) copy-start(bf16[1536,3]{0,1:T(4,128)(2,1)} %param.31) | copy-start | bytes 27652
  32.5 0.7 copy-start.6
  32.5 19.8 %copy-start.20 = (bf16[1536,32]{0,1:T(8,128)(2,1)S(1)}, bf16[1536,32]{0,1:T(8,128)(2,1)}, u32[]{:S(2)}) copy-start(bf16[1536,32]{0,1:T(8,128)(2,1)} %param.30) | copy-start | bytes 294916
  34.4 40.8 %all-to-all-start.1 = ((bf16[64,3,192]{2,1,0:T(4,128)(2,1)}), bf16[64,3,192]{2,1,0:T(4,128)(2,1)}, u32[]{:S(2)}, u32[]{:S(2)}) async-start(bf16[64,3,192]{2,1,0:T(4,128)(2,1)} %copy.98), calls=%async_computation.1 | async-start | bytes 262144 | tf_op jit(solution)/shard_map/all_to_all | solution.py:183
  51.0 1.8 copy-start.19
  52.3 17.1 %copy-start.17 = (f32[192]{0:T(256)S(1)}, f32[192]{0:T(256)}, u32[]{:S(2)}) copy-start(f32[192]{0:T(256)} %param.35) | copy-start | bytes 2308
  68.0 0.7 copy-start.5
  69.4 18.5 %copy-start.2 = (bf16[16,3,64,128]{3,2,1,0:T(8,128)(2,1)S(1)}, bf16[16,3,64,128]{3,2,1,0:T(8,128)(2,1)}, u32[]{:S(2)}) copy-start(bf16[16,3,64,128]{3,2,1,0:T(8,128)(2,1)} %param.25) | copy-start | bytes 2359300
  71.5 2.2 %copy-start.3 = (f32[16,16,3,64]{3,2,1,0:T(4,128)}, f32[16,16,3,64]{3,2,1,0:T(4,128)S(1)}, u32[]{:S(2)}) copy-start(f32[16,16,3,64]{3,2,1,0:T(4,128)S(1)} %reshape.238) | copy-start | bytes 589828
  75.2 23.6 %all-to-all-start.2 = ((bf16[64,3,256]{2,1,0:T(4,128)(2,1)}), bf16[64,3,256]{2,1,0:T(4,128)(2,1)S(1)}, u32[]{:S(2)}, u32[]{:S(2)}) async-start(bf16[64,3,256]{2,1,0:T(4,128)(2,1)} %copy.101), calls=%async_computation.2 | async-start | bytes 262144 | tf_op jit(solution)/shard_map/all_to_all | solution.py:184
  98.8 109.4 %all-to-all-start = ((bf16[64,3,64,128]{3,2,1,0:T(8,128)(2,1)}), bf16[64,3,64,128]{3,2,1,0:T(8,128)(2,1)}, u32[]{:S(2)}, u32[]{:S(2)}) async-start(bf16[64,3,64,128]{3,2,1,0:T(8,128)(2,1)} %bitcast.87), calls=%async_computation | async-start | bytes 6291456 | tf_op jit(solution)/shard_map/all_to_all | solution.py:182
  109.0 3.8 %copy-start.26 = (f32[3]{0:T(128)S(1)}, f32[3]{0:T(128)}, u32[]{:S(2)}) copy-start(f32[3]{0:T(128)} %param.38) | copy-start | bytes 40
  109.1 95.4 %all-reduce.3.cloned.1.call-start = ((), (), s32[]{:S(2)}) async-start(), calls=%async_computation.3 | async-start | bytes 1572864 | tf_op jit(solution)/shard_map/psum | solution.py:149
  110.7 2.1 copy-start.4
  110.7 2.1 copy-start.8
  110.7 2.1 copy-start.9
  112.9 16.8 %copy-start.24 = (f32[192]{0:T(256)S(1)}, f32[192]{0:T(256)}, u32[]{:S(2)}) copy-start(f32[192]{0:T(256)} %param.39) | copy-start | bytes 2308
  150.8 4.6 %copy-start.16 = (pred[1024]{0:T(1024)(128)(4,1)S(1)}, pred[1024]{0:T(1024)(128)(4,1)}, u32[]{:S(2)}) copy-start(pred[1024]{0:T(1024)(128)(4,1)} %get-tuple-element.28) | copy-start | bytes 3076
  150.8 4.6 %copy-start.18 = (pred[1024]{0:T(1024)(128)(4,1)S(1)}, pred[1024]{0:T(1024)(128)(4,1)}, u32[]{:S(2)}) copy-start(pred[1024]{0:T(1024)(128)(4,1)} %get-tuple-element.26) | copy-start | bytes 3076
  156.2 50.7 %copy-start.23 = (f32[1536]{0:T(1024)S(1)}, f32[1536]{0:T(1024)}, u32[]{:S(2)}) copy-start(f32[1536]{0:T(1024)} %param.41) | copy-start | bytes 18436
Sparse Core Ops, SparseCore 0:
  132.2 72.1 all-reduce.2
where the time goes:
time: 220 us
  waiting for transfers between devices  48.7 us (22%)
  blocking collectives  41 us (19%)
  starting transfers between devices  39.6 us (18%)
  other arithmetic  30.4 us (14%)
  local copies, waits for them, and re-layouts  22.8 us (10%)
  matrix products  22.6 us (10%)
  between operations  14.6 us (7%)
    psum x1, waiting for transfers between devices, local(): lax.psum(partial_sum.astype(jnp.bfloat16), 'narrow').astype(jnp.float32)  45.9 us
    another operation x3, other arithmetic  18.2 us
    all_to_all x1, starting transfers between devices, local(): lax.all_to_all(inner_bucket, 'wide', split_axis=0, concat_axis=0, tiled=T...  16.6 us
    psum x1, blocking collectives, local(): squares = lax.psum(jnp.sum(gated * gated, axis=1, keepdims=True), 'narrow')  14.5 us
    all_gather x1, blocking collectives, local(): full_rows = lax.all_gather(hidden, 'narrow', axis=1, tiled=True)  13.7 us
    all_gather x1, blocking collectives, local(): shared_in = lax.all_gather(shared_piece, 'narrow', axis=1, tiled=True)  12.7 us
    all_to_all x1, starting transfers between devices, local(): lax.all_to_all(shared_bucket, 'wide', split_axis=0, concat_axis=0, tiled=...  12.7 us
    all_to_all x1, starting transfers between devices, local(): lax.all_to_all(state_bucket, 'wide', split_axis=0, concat_axis=0, tiled=T...  10.3 us
  transfers between devices with their start and end apart: 4, of which 2 were waited for; matrix products, arithmetic and copies ran while one was open for 26% of the time, Pallas kernels for 0%

commit v1 on v0

--- a/solution.py
+++ b/solution.py
@@ -103,7 +103,9 @@
     wide_index = lax.axis_index("wide")
     wide_count = lax.axis_size("wide")
     narrow_count = lax.axis_size("narrow")
-    full_rows = lax.all_gather(hidden, "narrow", axis=1, tiled=True)
+    full_rows = jnp.concatenate(
+        lax.all_to_all(jnp.stack([hidden] * lax.axis_size("narrow")), "narrow", 0, 0), axis=1
+    )
     normed_in = root_norm(full_rows, input_gain)
     tokens = full_rows.shape[0]
     requests = start_state.shape[0]

time: 220 us -> 239 us (1.086)
  the two profiles are of different devices: /device:TPU:24 before, /device:TPU:8 now
where the time goes in v1:
time: 239 us; the launch traced here: 238 us
  waiting for transfers between devices  87.4 us (37%)
  starting transfers between devices  35.6 us (15%)
  other arithmetic  27.2 us (11%)
  blocking collectives  26 us (11%)
  local copies, waits for them, and re-layouts  24.3 us (10%)
  matrix products  23.1 us (10%)
  between operations  14.6 us (6%)
    psum x1, waiting for transfers between devices, local(): lax.psum(partial_sum.astype(jnp.bfloat16), 'narrow').astype(jnp.float32)  67.9 us
    another operation x3, other arithmetic  18.2 us
    all_to_all x1, starting transfers between devices, local(): lax.all_to_all(inner_bucket, 'wide', split_axis=0, concat_axis=0, tiled=T...  16.8 us
    psum x1, blocking collectives, local(): squares = lax.psum(jnp.sum(gated * gated, axis=1, keepdims=True), 'narrow')  13.2 us
    all_gather x1, blocking collectives, local(): shared_in = lax.all_gather(shared_piece, 'narrow', axis=1, tiled=True)  12.7 us
    all_to_all x1, waiting for transfers between devices, local(): lax.all_to_all(inner_bucket, 'wide', split_axis=0, concat_axis=0, tiled=T...  8.64 us
    all_to_all x1, starting transfers between devices, local(): lax.all_to_all(state_bucket, 'wide', split_axis=0, concat_axis=0, tiled=T...  8.13 us
    all_to_all x1, starting transfers between devices, local(): lax.all_to_all(shared_bucket, 'wide', split_axis=0, concat_axis=0, tiled=...  6.36 us
  transfers between devices with their start and end apart: 5, of which 4 were waited for; matrix products, arithmetic and copies ran while one was open for 24% of the time, Pallas kernels for 0%

profile of v1, /device:TPU:8, one launch (start us, length us, event | category | flops | bytes accessed | tf_op | source)
XLA Modules:
  0.0 238.2 jit_solution(11876830229013089312)
XLA Ops:
  7.2 1.9 stack.2
  9.1 4.3 %all-to-all-start = ((bf16[8,256,192]{1,2,0:T(8,128)(2,1)}), bf16[8,256,192]{1,2,0:T(8,128)(2,1)S(1)}, u32[]{:S(2)}, u32[]{:S(2)}) async-start(bf16[8,256,192]{1,2,0:T(8,128)(2,1)} %stack.2), calls=%async_computation | async-start | bytes 1572864 | tf_op jit(solution)/shard_map/all_to_all | solution.py:107
  13.5 0.6 gather_fusion
  14.5 4.5 %gather_fusion.2 = s32[1024]{0:T(1024)S(1)} fusion(s32[1024]{0:T(1024)S(1)} %copy-done.1, s32[1024]{0:T(1024)S(1)} %fusion.77), kind=kCustom, calls=%fused_computation.1.clone | custom fusion | bytes 12288 | tf_op jit(solution)/shard_map/jit(_take)/gather | solution.py:164
  19.0 0.6 broadcast_compare_fusion
  19.9 0.6 slice_convert_fusion.7
  20.5 6.0 %all-to-all-done = bf16[8,256,192]{1,2,0:T(8,128)(2,1)S(1)} async-done(((bf16[8,256,192]{1,2,0:T(8,128)(2,1)}), bf16[8,256,192]{1,2,0:T(8,128)(2,1)S(1)}, u32[]{:S(2)}, u32[]{:S(2)}) %all-to-all-start) | async-done | bytes 786464 | tf_op jit(solution)/shard_map/all_to_all | solution.py:107
  26.6 0.2 multiply_reduce_fusion
  26.9 1.4 multiply_convert_fusion
  28.2 0.2 fusion.11
  28.5 0.2 convolution_convert_fusion.11
  28.7 0.8 copy-done.8
  29.5 0.6 convolution_convert_fusion.4
  30.3 0.2 copy.81
  30.5 0.7 fusion.82
  31.2 0.2 copy.94
  31.7 0.8 copy.95
  32.6 12.7 %all_gather.3 = bf16[256,256]{0,1:T(8,128)(2,1)S(1)} all-gather(bf16[256,32]{0,1:T(8,128)(2,1)S(1)} %convolution_convert_fusion.11), channel_id=1, replica_groups=mesh['wide'=64,'narrow'=8] {'narrow'}, dimensions={1}, use_global_device_ids=true | all-gather | bytes 147456 | tf_op jit(solution)/shard_map/all_gather | solution.py:123
  45.4 0.2 convolution_convert_fusion.7
  45.7 0.3 convolution_convert_fusion.5
  46.0 0.7 copy.101
  46.7 0.1 slice.93
  46.8 0.2 convolution_convert_fusion.8
  47.0 0.3 convolution_convert_fusion.6
  47.3 0.7 copy.98
  48.1 16.8 %all-to-all-start.2 = ((bf16[64,3,192]{2,1,0:T(4,128)(2,1)}), bf16[64,3,192]{2,1,0:T(4,128)(2,1)}, u32[]{:S(2)}, u32[]{:S(2)}) async-start(bf16[64,3,192]{2,1,0:T(4,128)(2,1)} %copy.98), calls=%async_computation.2 | async-start | bytes 262144 | tf_op jit(solution)/shard_map/all_to_all | solution.py:185
  64.9 0.2 divide_multiply_fusion
  65.1 0.2 reshape.244
  65.3 1.4 broadcast_multiply_fusion
  66.7 1.5 divide_multiply_fusion.1
  68.2 8.6 %all-to-all-done.2 = bf16[64,3,192]{2,1,0:T(4,128)(2,1)} async-done(((bf16[64,3,192]{2,1,0:T(4,128)(2,1)}), bf16[64,3,192]{2,1,0:T(4,128)(2,1)}, u32[]{:S(2)}, u32[]{:S(2)}) %all-to-all-start.2) | async-done | bytes 73760 | tf_op jit(solution)/shard_map/all_to_all | solution.py:185
  76.9 6.4 %all-to-all-start.3 = ((bf16[64,3,256]{2,1,0:T(4,128)(2,1)}), bf16[64,3,256]{2,1,0:T(4,128)(2,1)}, u32[]{:S(2)}, u32[]{:S(2)}) async-start(bf16[64,3,256]{2,1,0:T(4,128)(2,1)} %copy.101), calls=%async_computation.3 | async-start | bytes 262144 | tf_op jit(solution)/shard_map/all_to_all | solution.py:186
  83.3 2.8 %add_convert_fusion = bf16[16,3,64,128]{3,2,1,0:T(8,128)(2,1)S(1)} fusion(bf16[16,3,64,128]{3,2,1,0:T(8,128)(2,1)S(1)} %copy-done.5, f32[16,3]{1,0:T(8,128)S(1)} %copy.93, f32[16,16,3,64]{3,2,1,0:T(4,128)S(1)} %broadcast_multiply_fusion, f32[16,16,256]{2,1,0:T(8,128)S(1)} %divide_multiply_fusion.1), kind=kOutput, calls=%fused_computation.14 | convolution fusion | flops 77070336 | bytes 2236416 | tf_op jit(solution)/shard_map/rsh,rshp,rsn->rhpn/dot_general | solution.py:73
  86.1 1.8 fusion.2
  87.8 2.5 %copy.114 = bf16[8,8,192,128]{3,2,1,0:T(8,128)(2,1)} copy(bf16[8,8,192,128]{3,1,2,0:T(8,128)(2,1)S(1)} %fusion.2) | data formatting | bytes 6291456
  90.3 4.8 %all-to-all-done.3 = bf16[64,3,256]{2,1,0:T(4,128)(2,1)} async-done(((bf16[64,3,256]{2,1,0:T(4,128)(2,1)}), bf16[64,3,256]{2,1,0:T(4,128)(2,1)}, u32[]{:S(2)}, u32[]{:S(2)}) %all-to-all-start.3) | async-done | bytes 98336 | tf_op jit(solution)/shard_map/all_to_all | solution.py:186
  95.1 8.1 %all-to-all-start.1 = ((bf16[64,3,64,128]{3,2,1,0:T(8,128)(2,1)}), bf16[64,3,64,128]{3,2,1,0:T(8,128)(2,1)}, u32[]{:S(2)}, u32[]{:S(2)}) async-start(bf16[64,3,64,128]{3,2,1,0:T(8,128)(2,1)} %bitcast.94), calls=%async_computation.1 | async-start | bytes 6291456 | tf_op jit(solution)/shard_map/all_to_all | solution.py:184
  103.3 18.0 %reduce-window.6 = s32[64,8,128]{2,1,0:T(8,128)S(1)} reduce-window(s32[64,8,128]{2,1,0:T(8,128)S(1)} %fusion.37, s32[]{:T(128)} %constant.71.clone.1), window={size=1x1x128 pad=0_0x0_0x127_0}, to_apply=%region_6.7 | reduce-window | flops 8323072 | bytes 524292 | tf_op jit(solution)/shard_map/reduce-window
  121.4 0.1 slice.102
  121.5 0.1 copy.91
  121.8 0.1 broadcast_add_fusion
  122.0 4.5 %gather_fusion.1 = s32[1024]{0:T(1024)S(1)} fusion(s32[1024]{0:T(1024)S(1)} %fusion.33, s32[1024]{0:T(1024)S(1)} %fusion.77), kind=kCustom, calls=%fused_computation.clone | custom fusion | bytes 12288 | tf_op jit(solution)/shard_map/jit(_take)/gather | solution.py:165
  126.6 0.8 convolution_convert_fusion.12
  127.4 0.2 copy.84
  127.6 1.6 copy.90
  129.3 0.2 copy.82
  129.4 0.3 fusion.55
  129.8 2.9 %convolution_multiply_fusion = f32[16,16,3,64]{3,1,2,0:T(8,128)S(1)} fusion(bf16[16,3,64,128]{3,2,1,0:T(8,128)(2,1)} %param.25, f32[16,16,3]{1,2,0:T(4,128)S(1)} %copy.82, f32[16,16,256]{2,1,0:T(8,128)S(1)} %divide_multiply_fusion.1), kind=kOutput, calls=%fused_computation.22 | convolution fusion | flops 75546624 | bytes 1146880 | tf_op jit(solution)/shard_map/rtn,rhpn->rthp/dot_general | solution.py:59
  132.7 0.6 fusion.10
  133.3 0.2 copy.89
  133.5 0.3 reshape.245
  133.9 0.2 multiply_reduce_fusion.1
  134.0 13.2 %psum.14 = f32[256,1]{0,1:T(1,128)S(1)} all-reduce(f32[256,1]{0,1:T(1,128)S(1)} %bitcast.104), channel_id=1, replica_groups=mesh['wide'=64,'narrow'=8] {'narrow'}, use_global_device_ids=true, to_apply=%region_3.4 | all-reduce | flops 256 | bytes 2048 | tf_op jit(solution)/shard_map/psum | solution.py:146
  147.3 2.5 %convolution_convert_fusion.2 = bf16[256,1536]{1,0:T(8,128)(2,1)} fusion(bf16[192,1536]{1,0:T(8,128)(2,1)} %param.40, f32[192]{0:T(256)S(1)} %copy-done.27, f32[256]{0:T(256)S(1)} %bitcast.113, f32[256,192]{1,0:T(8,128)S(1)} %reshape.245, bf16[256,384]{1,0:T(8,128)(2,1)S(1)} %copy-done.10), kind=kOutput, calls=%fused_computation.7 | convolution fusion | flops 151830528 | bytes 1771520 | tf_op jit(solution)/shard_map/dot_general | solution.py:150
  149.8 1.6 convolution_convert_fusion.10
  151.4 1.6 convolution_convert_fusion.9
  153.1 67.9 %all-reduce.3.cloned.1.call-done = bf16[256,1536]{1,0:T(8,128)(2,1)} async-done(((bf16[256,1536]{1,0:T(8,128)(2,1)}), bf16[256,1536]{1,0:T(8,128)(2,1)}) %all-reduce.3.cloned.1.call-update) | async-done | bytes 786448 | tf_op jit(solution)/shard_map/psum | solution.py:151
  221.0 1.5 fusion.3
  222.5 0.9 copy-done.11
  223.3 0.1 constant_dynamic-slice_fusion
  223.4 0.7 copy.103
  224.2 2.4 %convolution_convert_fusion.3 = bf16[256,403]{0,1:T(8,128)(2,1)} fusion(bf16[1536,403]{0,1:T(8,128)(2,1)S(1)} %copy-done, bf16[256,1536]{1,0:T(8,128)(2,1)} %copy-done.11, f32[1536]{0:T(1024)S(1)} %copy-done.26, f32[256]{0:T(256)S(1)} %add_rsqrt_fusion), kind=kOutput, calls=%fused_computation.23 | convolution fusion | flops 318608128 | bytes 2237952 | tf_op jit(solution)/shard_map/dot_general | solution.py:157
  226.6 3.7 %fusion.6 = bf16[2,8,192,128]{3,1,2,0:T(8,128)(2,1)S(1)} fusion(bf16[16,64]{1,0:T(8,128)(2,1)S(1)} %convolution_convert_fusion.12, bf16[8,8,192,128]{3,2,1,0:T(8,128)(2,1)} %bitcast.37), kind=kOutput, calls=%fused_computation.18 | convolution fusion | flops 50724864 | bytes 3934208 | tf_op jit(solution)/shard_map/dot_general | solution.py:200
  230.3 1.0 copy.116
  (94 shorter events, 1.8 us)
Async XLA Ops:
  7.2 217.0 %copy-start = (bf16[1536,403]{0,1:T(8,128)(2,1)S(1)}, bf16[1536,403]{0,1:T(8,128)(2,1)}, u32[]{:S(2)}) copy-start(bf16[1536,403]{0,1:T(8,128)(2,1)} %param.42) | copy-start | bytes 3714052
  7.2 6.2 %copy-start.16 = (s32[1024]{0:T(1024)S(1)}, s32[1024]{0:T(1024)}, u32[]{:S(2)}) copy-start(s32[1024]{0:T(1024)} %param.43) | copy-start | bytes 12292
  7.2 6.3 %copy-start.2 = (s32[1024]{0:T(1024)S(1)}, s32[1024]{0:T(1024)}, u32[]{:S(2)}) copy-start(s32[1024]{0:T(1024)} %param.44) | copy-start | bytes 12292
  7.2 7.2 %copy-start.1 = (s32[1024]{0:T(1024)S(1)}, s32[1024]{0:T(1024)}, u32[]{:S(2)}) copy-start(s32[1024]{0:T(1024)} %param.45) | copy-start | bytes 12292
  9.1 17.5 %all-to-all-start = ((bf16[8,256,192]{1,2,0:T(8,128)(2,1)}), bf16[8,256,192]{1,2,0:T(8,128)(2,1)S(1)}, u32[]{:S(2)}, u32[]{:S(2)}) async-start(bf16[8,256,192]{1,2,0:T(8,128)(2,1)} %stack.2), calls=%async_computation | async-start | bytes 1572864 | tf_op jit(solution)/shard_map/all_to_all | solution.py:107
  14.4 5.2 %copy-start.28 = (f32[3]{0:T(128)S(1)}, f32[3]{0:T(128)}, u32[]{:S(2)}) copy-start(f32[3]{0:T(128)} %param.33) | copy-start | bytes 40
  14.4 5.4 %copy-start.14 = (bf16[16,3,192]{2,0,1:T(8,128)(2,1)S(1)}, bf16[16,3,192]{2,0,1:T(8,128)(2,1)}, u32[]{:S(2)}) copy-start(bf16[16,3,192]{2,0,1:T(8,128)(2,1)} %param.26) | copy-start | bytes 55300
  14.4 5.4 %copy-start.15 = (bf16[16,3,256]{2,0,1:T(8,128)(2,1)S(1)}, bf16[16,3,256]{2,0,1:T(8,128)(2,1)}, u32[]{:S(2)}) copy-start(bf16[16,3,256]{2,0,1:T(8,128)(2,1)} %param.27) | copy-start | bytes 73732
  14.4 5.4 %copy-start.19 = (bf16[4,192]{1,0:T(4,128)(2,1)S(1)}, bf16[4,192]{1,0:T(4,128)(2,1)}, u32[]{:S(2)}) copy-start(bf16[4,192]{1,0:T(4,128)(2,1)} %param.34) | copy-start | bytes 4612
  14.5 5.4 %copy-start.20 = (bf16[4,256]{1,0:T(4,128)(2,1)S(1)}, bf16[4,256]{1,0:T(4,128)(2,1)}, u32[]{:S(2)}) copy-start(bf16[4,256]{1,0:T(4,128)(2,1)} %param.36) | copy-start | bytes 6148
  14.5 12.4 %copy-start.18 = (f32[1536]{0:T(1024)S(1)}, f32[1536]{0:T(1024)}, u32[]{:S(2)}) copy-start(f32[1536]{0:T(1024)} %param.28) | copy-start | bytes 18436
  19.7 27.3 %copy-start.21 = (s32[16]{0:T(128)}, s32[16]{0:T(128)S(1)}, u32[]{:S(2)}) copy-start(s32[16]{0:T(128)S(1)} %dynamic_slice.10) | copy-start | bytes 196
  26.8 1.4 copy-start.17
  26.9 1.6 copy-start.13
  28.2 1.3 copy-start.8
  28.5 1.8 copy-start.25
  30.1 18.0 %copy-start.9 = (bf16[256,384]{1,0:T(8,128)(2,1)}, bf16[256,384]{1,0:T(8,128)(2,1)S(1)}, u32[]{:S(2)}) copy-start(bf16[256,384]{1,0:T(8,128)(2,1)S(1)} %convolution_convert_fusion.4) | copy-start | bytes 589828
  30.5 34.4 %copy-start.23 = (f32[192]{0:T(256)S(1)}, f32[192]{0:T(256)}, u32[]{:S(2)}) copy-start(f32[192]{0:T(256)} %param.35) | copy-start | bytes 2308
  45.4 2.7 %copy-start.12 = (bf16[256,256]{1,0:T(8,128)(2,1)}, bf16[256,256]{1,0:T(8,128)(2,1)S(1)}, u32[]{:S(2)}) copy-start(bf16[256,256]{1,0:T(8,128)(2,1)S(1)} %copy.79) | copy-start | bytes 393220
  48.1 28.8 %all-to-all-start.2 = ((bf16[64,3,192]{2,1,0:T(4,128)(2,1)}), bf16[64,3,192]{2,1,0:T(4,128)(2,1)}, u32[]{:S(2)}, u32[]{:S(2)}) async-start(bf16[64,3,192]{2,1,0:T(4,128)(2,1)} %copy.98), calls=%async_computation.2 | async-start | bytes 262144 | tf_op jit(solution)/shard_map/all_to_all | solution.py:185
  64.9 18.4 %copy-start.5 = (bf16[16,3,64,128]{3,2,1,0:T(8,128)(2,1)S(1)}, bf16[16,3,64,128]{3,2,1,0:T(8,128)(2,1)}, u32[]{:S(2)}) copy-start(bf16[16,3,64,128]{3,2,1,0:T(8,128)(2,1)} %param.25) | copy-start | bytes 2359300
  65.3 20.7 %copy-start.6 = (f32[16,16,3,64]{3,2,1,0:T(4,128)}, f32[16,16,3,64]{3,2,1,0:T(4,128)S(1)}, u32[]{:S(2)}) copy-start(f32[16,16,3,64]{3,2,1,0:T(4,128)S(1)} %reshape.244) | copy-start | bytes 589828
  76.9 18.2 %all-to-all-start.3 = ((bf16[64,3,256]{2,1,0:T(4,128)(2,1)}), bf16[64,3,256]{2,1,0:T(4,128)(2,1)}, u32[]{:S(2)}, u32[]{:S(2)}) async-start(bf16[64,3,256]{2,1,0:T(4,128)(2,1)} %copy.101), calls=%async_computation.3 | async-start | bytes 262144 | tf_op jit(solution)/shard_map/all_to_all | solution.py:186
  95.1 131.5 %all-to-all-start.1 = ((bf16[64,3,64,128]{3,2,1,0:T(8,128)(2,1)}), bf16[64,3,64,128]{3,2,1,0:T(8,128)(2,1)}, u32[]{:S(2)}, u32[]{:S(2)}) async-start(bf16[64,3,64,128]{3,2,1,0:T(8,128)(2,1)} %bitcast.94), calls=%async_computation.1 | async-start | bytes 6291456 | tf_op jit(solution)/shard_map/all_to_all | solution.py:184
  103.3 117.7 %all-reduce.3.cloned.1.call-start = ((), (), s32[]{:S(2)}) async-start(), calls=%async_computation.4 | async-start | bytes 1572864 | tf_op jit(solution)/shard_map/psum | solution.py:151
  122.0 4.6 %copy-start.22 = (pred[1024]{0:T(1024)(128)(4,1)S(1)}, pred[1024]{0:T(1024)(128)(4,1)}, u32[]{:S(2)}) copy-start(pred[1024]{0:T(1024)(128)(4,1)} %get-tuple-element.28) | copy-start | bytes 3076
  122.0 4.6 %copy-start.24 = (pred[1024]{0:T(1024)(128)(4,1)S(1)}, pred[1024]{0:T(1024)(128)(4,1)}, u32[]{:S(2)}) copy-start(pred[1024]{0:T(1024)(128)(4,1)} %get-tuple-element.26) | copy-start | bytes 3076
  122.0 5.6 %copy-start.3 = (f32[8,256,192]{1,2,0:T(8,128)S(1)}, f32[8,256,192]{1,2,0:T(8,128)}, u32[]{:S(2)}) copy-start(f32[8,256,192]{1,2,0:T(8,128)} %get-tuple-element.34) | copy-start | bytes 4718596
  129.2 3.4 %copy-start.7 = (f32[16,16,3,64]{3,2,1,0:T(4,128)S(1)}, f32[16,16,3,64]{3,2,1,0:T(4,128)}, u32[]{:S(2)}) copy-start(f32[16,16,3,64]{3,2,1,0:T(4,128)} %copy-done.6) | copy-start | bytes 589828
  129.2 3.4 %copy-start.29 = (f32[3]{0:T(128)S(1)}, f32[3]{0:T(128)}, u32[]{:S(2)}) copy-start(f32[3]{0:T(128)} %param.38) | copy-start | bytes 40
  132.7 1.2 copy-start.10
  132.7 14.6 %copy-start.27 = (f32[192]{0:T(256)S(1)}, f32[192]{0:T(256)}, u32[]{:S(2)}) copy-start(f32[192]{0:T(256)} %param.39) | copy-start | bytes 2308
  147.3 73.7 %copy-start.4 = (f32[256,1536]{1,0:T(8,128)S(1)}, f32[256,1536]{1,0:T(8,128)}, u32[]{:S(2)}) copy-start(f32[256,1536]{1,0:T(8,128)} %copy.90) | copy-start | bytes 4718596
  153.1 71.1 %copy-start.26 = (f32[1536]{0:T(1024)S(1)}, f32[1536]{0:T(1024)}, u32[]{:S(2)}) copy-start(f32[1536]{0:T(1024)} %param.41) | copy-start | bytes 18436
  222.5 0.9 copy-start.11
Sparse Core Ops, SparseCore 0:
  149.9 71.0 all-reduce.2
